TPU v7x, 128 devices: a whole 4x4x4 slice. The times are simulated.
128 devices in a mesh: row: 8 (over y, z_lo), col: 16 (over z_hi, x, core).
Axes of the slice: x: 4, y: 4, z: 4 (z_hi: 2, z_lo: 2; z = z_hi * 2 + z_lo), core: 2. Of those that a mesh axis runs over, the one named last changes fastest.
Arguments:
- kernel: bfloat16 [20480, 20480], P('row', 'col'), may hold values from -2.861023e-06 to 2.861023e-06
- occ: bfloat16 [20480, 128], P(('row', 'col')), may hold values from -6 to 6
- virt: bfloat16 [20480, 512], P(('col', 'row')), may hold values from -6 to 6
- rhs: float32 [128, 512], replicated, may hold values from -6 to 6
- e_occ: float32 [128], replicated, may hold values from -2 to -0.5
- e_virt: float32 [512], replicated, may hold values from 0.2 to 3
Outputs:
- amplitudes: float32 [128, 512], replicated
All inputs are finite; a program needn't handle non-finite values.
Results may differ from a plain program's by a relative error of at most 0.0045.
Values may be sent and summed in bfloat16 or wider, within the bound.
No kernel may reach another device: no remote copies, remote signals or barrier semaphores. Data moves between devices by JAX's collectives and lax.ppermute only.
A program may use at most 64 MiB of HBM per device.

v0:
```python
import math
import jax
import jax.numpy as jnp
from jax import lax
from jax.sharding import PartitionSpec as P

ITERS = 2


def in_order(pieces, dim):
    pieces = jnp.moveaxis(pieces, 0, dim)
    dims = pieces.shape
    return pieces.reshape(*dims[:dim], dims[dim] * dims[dim + 1], *dims[dim + 2 :])


def sent_to_all(shard, axis):
    peers = lax.axis_size(axis)
    return lax.all_to_all(
        jnp.broadcast_to(shard[None], (peers, *shard.shape)), axis, 0, 0, tiled=True
    )


def gather_directly(shard, axis, dim):
    return in_order(sent_to_all(shard, axis), dim)


def body(kernel, occ, virt, rhs, e_occ, e_virt):
    denom = e_virt[None, :] - e_occ[:, None]
    amplitudes = rhs / denom
    virt_cols = gather_directly(virt, "row", 0)
    occ_full = lax.all_gather(occ, "col", axis=0, tiled=True)

    def fold(total, pieces, start):
        resp_rows, occ_piece = pieces
        kern_rows = lax.dynamic_slice_in_dim(kernel, start, resp_rows.shape[0], 0)
        outer = lax.dot_general(
            resp_rows, virt_cols, (((1,), (1,)), ((), ())), preferred_element_type=jnp.float32
        )
        weighted = (kern_rows.astype(jnp.float32) * outer).astype(jnp.bfloat16)
        return total + lax.dot_general(
            occ_piece, weighted, (((0,), (0,)), ((), ())), preferred_element_type=jnp.float32
        )

    for step in range(ITERS):
        amp_b = amplitudes.astype(jnp.bfloat16)
        empty = jnp.zeros((occ.shape[1], virt_cols.shape[0]), jnp.float32)
        resp_full = jnp.dot(occ_full, amp_b, preferred_element_type=jnp.float32).astype(
            jnp.bfloat16
        )
        height = occ_full.shape[0]
        block = math.gcd(height, 512)

        def add_block(index, total):
            start = (index * block).astype(jnp.int32)
            pieces = (
                lax.dynamic_slice_in_dim(resp_full, start, block, 0),
                lax.dynamic_slice_in_dim(occ_full, start, block, 0),
            )
            return fold(total, pieces, start)

        partial_sum = lax.fori_loop(0, height // block, add_block, empty)
        projection = jnp.dot(
            partial_sum, virt_cols.astype(jnp.float32), precision=lax.Precision.HIGHEST
        )
        exchange = lax.psum(projection, ("row", "col"))
        amplitudes = (rhs - exchange) / denom
    return amplitudes


def solution(mesh):
    in_specs = (P("row", "col"), P(("row", "col"), None), P(("col", "row"), None), P(), P(), P())
    out_specs = P()
    return jax.shard_map(body, mesh=mesh, in_specs=in_specs, out_specs=out_specs, check_vma=False)
```

profile of v0, /device:TPU:1, one launch (start us, length us, event | category | flops | bytes accessed | tf_op | source)
XLA Modules:
  0.0 371.0 jit_solution(7374602793152194372)
XLA Ops:
  6.5 0.0 copy-start.1
  6.5 0.0 copy-start
  6.5 0.0 copy-start.3
  6.5 0.0 copy-start.2
  6.5 2.1 broadcast_in_dim.2
  8.7 6.4 %all-to-all-start = ((bf16[8,160,512]{2,1,0:T(8,128)(2,1)}), bf16[8,160,512]{2,1,0:T(8,128)(2,1)S(1)}, u32[]{:S(2)}, u32[]{:S(2)}) async-start(bf16[8,160,512]{2,1,0:T(8,128)(2,1)} %broadcast_in_dim.2), calls=%async_computation | async-start | bytes 2621440 | tf_op jit(solution)/shard_map/all_to_all | solution.py:18
  15.0 0.0 all-reduce.3.cloned.1.call-start
  15.1 0.0 copy-done.1
  15.1 28.9 %all_gather.3 = bf16[2560,128]{1,0:T(8,128)(2,1)S(1)} all-gather(bf16[160,128]{1,0:T(8,128)(2,1)S(1)} %copy-done.1), channel_id=1, replica_groups=mesh['row'=8,'col'=16] {'col'}, dimensions={0}, use_global_device_ids=true | all-gather | bytes 696320 | tf_op jit(solution)/shard_map/all_gather | solution.py:31
  44.0 0.0 copy-done
  44.0 0.0 copy-done.3
  44.0 0.0 copy-done.2
  44.0 2.4 fusion.14
  46.5 0.0 all-to-all-done
  46.5 14.5 %while.28 = (s32[]{:T(128)}, f32[128,1280]{1,0:T(8,128)S(1)}, bf16[2560,128]{1,0:T(8,128)(2,1)S(1)}, bf16[2560,1280]{1,0:T(8,128)(2,1)}, bf16[2560,512]{1,0:T(8,...) while((s32[]{:T(128)}, f32[128,1280]{1,0:T(8,128)S(1)}, ...), condition=%wide.region_1.0_spmd.clone, body=%wide.region_0.0_spmd.clone.sunk | while | flops 841154560 | bytes 4589724 | solution.py:61
  46.5 2.9 convolution_add_fusion.4
  49.4 2.9 convolution_add_fusion.4
  52.3 2.9 convolution_add_fusion.4
  55.2 2.9 convolution_add_fusion.4
  58.1 2.9 convolution_add_fusion.4
  61.0 1.4 fusion.24
  62.4 0.0 all-reduce.3.cloned.1.call-update
  62.4 0.0 all-reduce.5.cloned.1.call-start
  62.5 139.9 %all-reduce.3.cloned.1.call-done = f32[128,512]{1,0:T(8,128)} async-done(((f32[128,512]{1,0:T(8,128)}), f32[128,512]{1,0:T(8,128)}) %all-reduce.3.cloned.1.call-update) | async-done | bytes 262160 | tf_op jit(solution)/shard_map/psum | solution.py:65
  202.4 3.4 fusion.15
  205.8 14.5 %while.29 = (s32[]{:T(128)}, f32[128,1280]{1,0:T(8,128)S(1)}, bf16[2560,128]{1,0:T(8,128)(2,1)S(1)}, bf16[2560,1280]{1,0:T(8,128)(2,1)}, bf16[2560,512]{1,0:T(8,...) while((s32[]{:T(128)}, f32[128,1280]{1,0:T(8,128)S(1)}, ...), condition=%wide.region_4.0_spmd.clone, body=%wide.region_3.0_spmd.clone.sunk | while | flops 841154560 | bytes 4589724 | solution.py:61
  205.8 2.9 convolution_add_fusion.5
  208.7 2.9 convolution_add_fusion.5
  211.6 2.9 convolution_add_fusion.5
  214.5 2.9 convolution_add_fusion.5
  217.4 2.9 convolution_add_fusion.5
  220.3 1.4 fusion.25
  221.7 0.0 all-reduce.5.cloned.1.call-update
  221.7 140.7 %all-reduce.5.cloned.1.call-done = f32[128,512]{1,0:T(8,128)} async-done(((f32[128,512]{1,0:T(8,128)}), f32[128,512]{1,0:T(8,128)}) %all-reduce.5.cloned.1.call-update) | async-done | bytes 262160 | tf_op jit(solution)/shard_map/psum | solution.py:65
  362.4 1.8 subtract_divide_fusion
  (2 shorter events, 0.0 us)
Async XLA Ops:
  6.5 8.6 %copy-start.1 = (bf16[160,128]{1,0:T(8,128)(2,1)S(1)}, bf16[160,128]{1,0:T(8,128)(2,1)}, u32[]{:S(2)}) copy-start(bf16[160,128]{1,0:T(8,128)(2,1)} %param.11) | copy-start | bytes 122884
  6.5 37.5 %copy-start = (f32[128,512]{1,0:T(8,128)S(1)}, f32[128,512]{1,0:T(8,128)}, u32[]{:S(2)}) copy-start(f32[128,512]{1,0:T(8,128)} %param.13) | copy-start | bytes 786436
  6.5 37.5 %copy-start.3 = (f32[128]{0:T(128)S(1)}, f32[128]{0:T(128)}, u32[]{:S(2)}) copy-start(f32[128]{0:T(128)} %param.14) | copy-start | bytes 1540
  6.5 37.5 %copy-start.2 = (f32[512]{0:T(512)S(1)}, f32[512]{0:T(512)}, u32[]{:S(2)}) copy-start(f32[512]{0:T(512)} %param.15) | copy-start | bytes 6148
  8.7 37.8 %all-to-all-start = ((bf16[8,160,512]{2,1,0:T(8,128)(2,1)}), bf16[8,160,512]{2,1,0:T(8,128)(2,1)S(1)}, u32[]{:S(2)}, u32[]{:S(2)}) async-start(bf16[8,160,512]{2,1,0:T(8,128)(2,1)} %broadcast_in_dim.2), calls=%async_computation | async-start | bytes 2621440 | tf_op jit(solution)/shard_map/all_to_all | solution.py:18
  15.0 187.4 %all-reduce.3.cloned.1.call-start = ((), (), s32[]{:S(2)}) async-start(), calls=%async_computation.1 | async-start | bytes 524288 | tf_op jit(solution)/shard_map/psum | solution.py:65
  62.4 300.0 %all-reduce.5.cloned.1.call-start = ((), (), s32[]{:S(2)}) async-start(), calls=%async_computation.2 | async-start | bytes 524288 | tf_op jit(solution)/shard_map/psum | solution.py:65
Sparse Core Ops, SparseCore 0:
  62.5 139.8 all-reduce.2
  221.9 140.5 all-reduce.4
where the time goes:
time: 372 us; the launch traced here: 371 us
  waiting for transfers between devices  281 us (76%)
  matrix products  37.4 us (10%)
  blocking collectives  28.9 us (8%)
  between operations  13.5 us (4%)
  starting transfers between devices  6.44 us (2%)
    psum x2, waiting for transfers between devices, body(): exchange = lax.psum(projection, ('row', 'col'))  281 us
    all_gather x1, blocking collectives, body(): occ_full = lax.all_gather(occ, 'col', axis=0, tiled=True)  28.9 us
    dot_general x10, matrix products, fold(): lax.dot_general(occ_piece, weighted, (((0,), (0,)), ((), ())), preferred_...  28.8 us
  transfers between devices with their start and end apart: 3, of which 2 were waited for; matrix products, arithmetic and copies ran while one was open for 1% of the time, Pallas kernels for 0%

commit v1 on v0

--- a/solution.py
+++ b/solution.py
@@ -62,7 +62,7 @@
         projection = jnp.dot(
             partial_sum, virt_cols.astype(jnp.float32), precision=lax.Precision.HIGHEST
         )
-        exchange = lax.psum(projection, ("row", "col"))
+        exchange = jnp.sum(lax.all_gather(projection, ("row", "col")), axis=0)
         amplitudes = (rhs - exchange) / denom
     return amplitudes
 

time: 372 us -> 575 us (1.55)
  waiting for transfers between devices: 281 us -> 462 us
  other arithmetic: 1.76 us -> 24.8 us
    all_gather x0 -> x2, waiting for transfers between devices: none -> 462 us  [body(): exchange = jnp.sum(lax.all_gather(projection, ('row', 'col')), axis=0)]
    psum x2 -> x0, waiting for transfers between devices: 281 us -> none  [body(): exchange = lax.psum(projection, ('row', 'col'))]
    reduce_sum x0 -> x2, other arithmetic: none -> 24 us  [body(): exchange = jnp.sum(lax.all_gather(projection, ('row', 'col')), axis=0)]
  transfers between devices with their start and end apart: 3 -> 3, of which waited for: 2 -> 2; matrix products, arithmetic and copies ran while one was open for 1% -> 0% of each run, Pallas kernels for 0% -> 0%
where the time goes in v1:
time: 575 us
  waiting for transfers between devices  462 us (80%)
  matrix products  36.5 us (6%)
  blocking collectives  28.9 us (5%)
  other arithmetic  24.8 us (4%)
  between operations  13.5 us (2%)
  starting transfers between devices  6.44 us (1%)
    all_gather x2, waiting for transfers between devices, body(): exchange = jnp.sum(lax.all_gather(projection, ('row', 'col')), axis=0)  462 us
    all_gather x1, blocking collectives, body(): occ_full = lax.all_gather(occ, 'col', axis=0, tiled=True)  28.9 us
    dot_general x10, matrix products, fold(): lax.dot_general(occ_piece, weighted, (((0,), (0,)), ((), ())), preferred_...  28.8 us
    reduce_sum x2, other arithmetic, body(): exchange = jnp.sum(lax.all_gather(projection, ('row', 'col')), axis=0)  24 us
  transfers between devices with their start and end apart: 3, of which 2 were waited for; matrix products, arithmetic and copies ran while one was open for 0% of the time, Pallas kernels for 0%

profile of v1, /device:TPU:1, one launch (start us, length us, event | category | flops | bytes accessed | tf_op | source)
XLA Modules:
  0.0 574.9 jit_solution(15960842556876951890)
XLA Ops:
  6.5 0.0 copy-start.1
  6.5 0.0 copy-start
  6.5 0.0 copy-start.3
  6.5 0.0 copy-start.2
  6.5 2.1 broadcast_in_dim.2
  8.7 6.4 %all-to-all-start = ((bf16[8,160,512]{2,1,0:T(8,128)(2,1)}), bf16[8,160,512]{2,1,0:T(8,128)(2,1)S(1)}, u32[]{:S(2)}, u32[]{:S(2)}) async-start(bf16[8,160,512]{2,1,0:T(8,128)(2,1)} %broadcast_in_dim.2), calls=%async_computation | async-start | bytes 2621440 | tf_op jit(solution)/shard_map/all_to_all | solution.py:18
  15.0 0.0 all-gather.5.cloned.1.call-start
  15.1 0.0 copy-done.1
  15.1 28.9 %all_gather.15 = bf16[2560,128]{1,0:T(8,128)(2,1)S(1)} all-gather(bf16[160,128]{1,0:T(8,128)(2,1)S(1)} %copy-done.1), channel_id=1, replica_groups=mesh['row'=8,'col'=16] {'col'}, dimensions={0}, use_global_device_ids=true | all-gather | bytes 696320 | tf_op jit(solution)/shard_map/all_gather | solution.py:31
  44.0 0.0 copy-done
  44.0 0.0 copy-done.3
  44.0 0.0 copy-done.2
  44.0 2.4 fusion.14
  46.5 0.0 all-to-all-done
  46.5 14.5 %while.28 = (s32[]{:T(128)}, f32[128,1280]{1,0:T(8,128)S(1)}, bf16[2560,128]{1,0:T(8,128)(2,1)S(1)}, bf16[2560,1280]{1,0:T(8,128)(2,1)}, bf16[2560,512]{1,0:T(8,...) while((s32[]{:T(128)}, f32[128,1280]{1,0:T(8,128)S(1)}, ...), condition=%wide.region_1.0_spmd.clone, body=%wide.region_0.0_spmd.clone.sunk | while | flops 841154560 | bytes 4589724 | solution.py:61
  46.5 2.9 convolution_add_fusion.4
  49.4 2.9 convolution_add_fusion.4
  52.3 2.9 convolution_add_fusion.4
  55.2 2.9 convolution_add_fusion.4
  58.1 2.9 convolution_add_fusion.4
  61.0 1.4 fusion.24
  62.4 0.0 all-gather.5.cloned.1.call-update
  62.4 0.0 all-gather.7.cloned.1.call-start
  62.5 230.2 %all-gather.5.cloned.1.call-done = f32[16384,512]{1,0:T(8,128)} async-done(((f32[128,512]{1,0:T(8,128)}), f32[16384,512]{1,0:T(8,128)}) %all-gather.5.cloned.1.call-update) | async-done | bytes 33554448 | tf_op jit(solution)/shard_map/all_gather | solution.py:65
  292.7 12.0 %reduce_sum.18 = f32[128,512]{1,0:T(8,128)S(1)} reduce(f32[128,128,512]{2,1,0:T(8,128)} %bitcast.19, f32[]{:T(128)} %constant.60.clone.1), dimensions={0}, to_apply=%region_2.0 | reduce | flops 8323072 | bytes 33816580 | tf_op jit(solution)/shard_map/reduce_sum | solution.py:65
  304.7 2.4 fusion.15
  307.1 14.5 %while.29 = (s32[]{:T(128)}, f32[128,1280]{1,0:T(8,128)S(1)}, bf16[2560,128]{1,0:T(8,128)(2,1)S(1)}, bf16[2560,1280]{1,0:T(8,128)(2,1)}, bf16[2560,512]{1,0:T(8,...) while((s32[]{:T(128)}, f32[128,1280]{1,0:T(8,128)S(1)}, ...), condition=%wide.region_4.0_spmd.clone, body=%wide.region_3.0_spmd.clone.sunk | while | flops 841154560 | bytes 4589724 | solution.py:61
  307.1 2.9 convolution_add_fusion.5
  310.0 2.9 convolution_add_fusion.5
  312.9 2.9 convolution_add_fusion.5
  315.8 2.9 convolution_add_fusion.5
  318.7 2.9 convolution_add_fusion.5
  321.6 1.4 fusion.25
  323.0 0.0 all-gather.7.cloned.1.call-update
  323.1 232.2 %all-gather.7.cloned.1.call-done = f32[16384,512]{1,0:T(8,128)} async-done(((f32[128,512]{1,0:T(8,128)}), f32[16384,512]{1,0:T(8,128)}) %all-gather.7.cloned.1.call-update) | async-done | bytes 33554448 | tf_op jit(solution)/shard_map/all_gather | solution.py:65
  555.2 12.0 %reduce_sum.19 = f32[128,512]{1,0:T(8,128)S(1)} reduce(f32[128,128,512]{2,1,0:T(8,128)} %bitcast.20, f32[]{:T(128)} %constant.60.clone.1), dimensions={0}, to_apply=%region_5.0 | reduce | flops 8323072 | bytes 33816580 | tf_op jit(solution)/shard_map/reduce_sum | solution.py:65
  567.2 0.8 subtract_divide_fusion
  (2 shorter events, 0.0 us)
Async XLA Ops:
  6.5 8.6 %copy-start.1 = (bf16[160,128]{1,0:T(8,128)(2,1)S(1)}, bf16[160,128]{1,0:T(8,128)(2,1)}, u32[]{:S(2)}) copy-start(bf16[160,128]{1,0:T(8,128)(2,1)} %param.11) | copy-start | bytes 122884
  6.5 37.5 %copy-start = (f32[128,512]{1,0:T(8,128)S(1)}, f32[128,512]{1,0:T(8,128)}, u32[]{:S(2)}) copy-start(f32[128,512]{1,0:T(8,128)} %param.13) | copy-start | bytes 786436
  6.5 37.5 %copy-start.3 = (f32[128]{0:T(128)S(1)}, f32[128]{0:T(128)}, u32[]{:S(2)}) copy-start(f32[128]{0:T(128)} %param.14) | copy-start | bytes 1540
  6.5 37.5 %copy-start.2 = (f32[512]{0:T(512)S(1)}, f32[512]{0:T(512)}, u32[]{:S(2)}) copy-start(f32[512]{0:T(512)} %param.15) | copy-start | bytes 6148
  8.7 37.8 %all-to-all-start = ((bf16[8,160,512]{2,1,0:T(8,128)(2,1)}), bf16[8,160,512]{2,1,0:T(8,128)(2,1)S(1)}, u32[]{:S(2)}, u32[]{:S(2)}) async-start(bf16[8,160,512]{2,1,0:T(8,128)(2,1)} %broadcast_in_dim.2), calls=%async_computation | async-start | bytes 2621440 | tf_op jit(solution)/shard_map/all_to_all | solution.py:18
  15.0 277.6 %all-gather.5.cloned.1.call-start = ((), (), s32[]{:S(2)}) async-start(), calls=%async_computation.1 | async-start | bytes 33816576 | tf_op jit(solution)/shard_map/all_gather | solution.py:65
  62.4 492.8 %all-gather.7.cloned.1.call-start = ((), (), s32[]{:S(2)}) async-start(), calls=%async_computation.2 | async-start | bytes 33816576 | tf_op jit(solution)/shard_map/all_gather | solution.py:65
Sparse Core Ops, SparseCore 0:
  62.5 230.0 all-gather.4
  323.2 232.0 all-gather.6
